TPU v7x, 32 devices: a whole 2x2x4 slice. The times are simulated.
32 devices in a mesh: expert: 4 (over y, core), dp: 8 (over z, x).
Axes of the slice: x: 2, y: 2, z: 4, core: 2. Of those that a mesh axis runs over, the one named last changes fastest.
Arguments:
- tokens: bfloat16 [32768, 2048], P(('expert', 'dp')), may hold values from -6 to 6
- block_expert: int32 [256, 1], P(('expert', 'dp')), may hold values from 0 to 3; in each aligned block of 8 rows (0 to 7, 8 to 15, ...) at most 4 rows name the same one
- gate_weight: bfloat16 [4, 2048, 768], P('expert', 'dp'), may hold values from -0.125 to 0.125
- up_weight: bfloat16 [4, 2048, 768], P('expert', 'dp'), may hold values from -0.125 to 0.125
- down_weight: bfloat16 [4, 768, 2048], P('expert', None, 'dp'), may hold values from -0.21875 to 0.21875
Outputs:
- r_factor: float32 [4, 768, 768], P('expert', 'dp')
- compressed_down: float32 [4, 768, 2048], P('expert', None, 'dp')
Inputs may be any that keep to these rules, and one draw needn't show every extreme that they name: `block_expert`: among the 8 blocks of one device, at most 4 name the same expert, and in every draw some device has exactly 4 blocks for one expert.
All inputs are finite; a program needn't handle non-finite values.
Results may differ from a plain program's by a relative error of at most 0.0003.
Values may be sent and summed in bfloat16 or wider, within the bound.
No kernel may reach another device: no remote copies, remote signals or barrier semaphores. Data moves between devices by JAX's collectives and lax.ppermute only.
A program may use at most 128 MiB of HBM per device.

v0:
```python
import jax
import jax.numpy as jnp
from jax import lax
from jax.sharding import PartitionSpec as P

BROWS = 128


damping = 0.05


def on_device(tokens, block_expert, gate_weight, up_weight, down_weight):
    n_expert = lax.axis_size("expert")
    n_data = lax.axis_size("dp")
    exp_local = gate_weight.shape[0]
    width = gate_weight.shape[2]
    model = tokens.shape[1]
    experts = exp_local * n_expert
    blk_count = block_expert.shape[0]
    capacity = max(2, 2 * blk_count // experts)
    rows_avg = blk_count * BROWS * n_data * n_expert // experts
    blocks = tokens.reshape(blk_count, BROWS, model)
    ids = block_expert[:, 0]
    positions = jnp.arange(blk_count, dtype=jnp.int32)
    same = ids[:, None] == ids[None, :]
    earlier = positions[None, :] < positions[:, None]
    ranks = jnp.sum((same & earlier).astype(jnp.int32), axis=1)
    slots = jnp.arange(experts * capacity, dtype=jnp.int32)
    match = (ids[None, :] == (slots // capacity)[:, None]) & (
        ranks[None, :] == (slots % capacity)[:, None]
    )
    found = jnp.sum(match.astype(jnp.int32), axis=1)
    source = jnp.sum(match.astype(jnp.int32) * positions[None, :], axis=1) + (1 - found) * blk_count
    padded = jnp.concatenate([blocks, jnp.zeros((1, BROWS, model), jnp.bfloat16)], axis=0)
    outgoing = padded[source].reshape(n_expert, exp_local, capacity, BROWS, model)
    arrived = lax.all_to_all(outgoing, "expert", split_axis=0, concat_axis=0, tiled=True)
    eye = jnp.eye(width, dtype=jnp.float32)
    my_rows = width // n_data
    rows = arrived[:, 0].reshape(-1, model)
    gate = jnp.dot(
        rows,
        lax.all_gather(gate_weight[0], "dp", axis=0, tiled=True),
        preferred_element_type=jnp.float32,
    )
    lifted = jnp.dot(
        rows,
        lax.all_gather(up_weight[0], "dp", axis=0, tiled=True),
        preferred_element_type=jnp.float32,
    )
    hidden = jax.nn.silu(gate) * lifted
    gram = jnp.dot(hidden.T, hidden, precision=lax.Precision.HIGHEST) / float(rows_avg)
    total = lax.psum(gram, "dp") + damping * eye
    upper = jnp.linalg.cholesky(total).T
    factors = [lax.dynamic_slice_in_dim(upper, lax.axis_index("dp") * my_rows, my_rows, 0)]
    products = [jnp.dot(upper, down_weight[0].astype(jnp.float32), precision=lax.Precision.HIGHEST)]
    return (jnp.stack(factors), jnp.stack(products))


def solution(mesh):
    placed = (
        P(("expert", "dp"), None),
        P(("expert", "dp"), None),
        P("expert", "dp", None),
        P("expert", "dp", None),
        P("expert", None, "dp"),
    )
    return jax.shard_map(
        on_device,
        mesh=mesh,
        in_specs=placed,
        out_specs=(P("expert", "dp", None), P("expert", None, "dp")),
        check_vma=False,
    )
```

profile of v0, /device:TPU:0, one launch (start us, length us, event | category | flops | bytes accessed | tf_op | source)
XLA Modules:
  0.0 432.7 jit_solution(1642863032886914557)
XLA Ops:
  7.9 5.0 %concatenate.3 = bf16[9,128,2048]{2,1,0:T(8,128)(2,1)} pad(bf16[8,128,2048]{2,1,0:T(8,128)(2,1)} %bitcast.59, bf16[]{:T(256)} %constant.236.clone.1), padding=0_1x0_0x0_0 | pad | bytes 8912898 | tf_op jit(solution)/shard_map/concatenate | solution.py:34
  13.2 7.1 %gather_fusion = bf16[16,128,2048]{2,1,0:T(8,128)(2,1)} fusion(bf16[9,128,2048]{2,1,0:T(8,128)(2,1)} %concatenate.3, s32[1024]{0:T(1024)S(1)} %pad_clamp_fusion), kind=kCustom, calls=%fused_computation | custom fusion | bytes 16777280 | tf_op jit(solution)/shard_map/gather | solution.py:35
  20.3 5.7 %all-to-all-start = ((bf16[4,1,4,128,2048]{4,3,2,1,0:T(8,128)(2,1)}), bf16[4,1,4,128,2048]{4,3,2,1,0:T(8,128)(2,1)}, u32[]{:S(2)}, u32[]{:S(2)}) async-start(bf16[4,1,4,128,2048]{4,3,2,1,0:T(8,128)(2,1)} %bitcast.58), calls=%async_computation | async-start | bytes 16777216 | tf_op jit(solution)/shard_map/all_to_all | solution.py:36
  26.7 46.2 %all-gather.7.cloned.1.call-done = bf16[1,2048,768]{2,1,0:T(8,128)(2,1)} async-done(((bf16[1,256,768]{2,1,0:T(8,128)(2,1)}), bf16[1,2048,768]{2,1,0:T(8,128)(2,1)}) %all-gather.7.cloned.1.call-update) | async-done | bytes 3145744 | tf_op jit(solution)/shard_map/all_gather | solution.py:47
  72.9 46.9 %all-to-all-done = bf16[4,1,4,128,2048]{4,3,2,1,0:T(8,128)(2,1)} async-done(((bf16[4,1,4,128,2048]{4,3,2,1,0:T(8,128)(2,1)}), bf16[4,1,4,128,2048]{4,3,2,1,0:T(8,128)(2,1)}, u32[]{:S(2)}, u32[]{:S(2)}) %all-to-all-start) | async-done | bytes 8388640 | tf_op jit(solution)/shard_map/all_to_all | solution.py:36
  119.8 11.7 %fusion.7 = f32[2048,768]{1,0:T(8,128)} fusion(bf16[2048,2048]{1,0:T(8,128)(2,1)} %bitcast.5, bf16[1,2048,768]{2,1,0:T(8,128)(2,1)} %all-gather.7.cloned.1.call-done), kind=kOutput, calls=%fused_computation.8 | convolution fusion | flops 6442450944 | bytes 17825792 | tf_op jit(solution)/shard_map/dot_general | solution.py:45
  131.5 2.3 all-gather.5.cloned.1.call-done
  133.8 10.3 %fusion.9 = f32[2048,768]{1,0:T(8,128)S(1)} fusion(bf16[2048,2048]{1,0:T(8,128)(2,1)} %bitcast.5, bf16[1,2048,768]{2,1,0:T(8,128)(2,1)} %all-gather.5.cloned.1.call-done), kind=kOutput, calls=%fused_computation.10 | convolution fusion | flops 6442450944 | bytes 17825792 | tf_op jit(solution)/shard_map/dot_general | solution.py:40
  144.2 20.1 %fusion.13 = f32[768,768]{0,1:T(8,128)} fusion(f32[2048,768]{1,0:T(8,128)S(1)} %copy-done.4, f32[2048,768]{1,0:T(8,128)S(1)} %fusion.9), kind=kOutput, calls=%fused_computation.19 | convolution fusion | flops 14503968768 | bytes 14942208 | tf_op jit(solution)/shard_map/dot_general | solution.py:51
  164.2 107.7 %all-reduce.4.cloned.1.call-done = f32[768,768]{0,1:T(8,128)} async-done(((f32[768,768]{0,1:T(8,128)}), f32[768,768]{0,1:T(8,128)}) %all-reduce.4.cloned.1.call-update) | async-done | bytes 2359312 | tf_op jit(solution)/shard_map/psum | solution.py:52
  272.0 3.3 select_add_fusion
  275.2 3.2 copy.24
  281.8 11.7 %cholesky.164 = f32[128,128]{1,0:T(8,128)S(1)} custom-call(f32[128,128]{1,0:T(8,128)S(1)} %cholesky.421), custom_call_target="Cholesky" | custom-call | tf_op jit(solution)/shard_map/jit(cholesky)/cholesky | solution.py:53
  293.7 9.8 %custom-call.43 = f32[1,128,128]{1,2,0:T(8,128)S(1)} custom-call(f32[1,128,128]{2,1,0:T(8,128)S(1)} %get-tuple-element.13), custom_call_target="InvertDiagBlocksLowerTriangular" | custom-call | tf_op jit(solution)/shard_map/jit(cholesky)/cholesky | solution.py:53
  306.8 11.7 %cholesky.187 = f32[128,128]{1,0:T(8,128)S(1)} custom-call(f32[128,128]{1,0:T(8,128)S(1)} %cholesky.425), custom_call_target="Cholesky" | custom-call | tf_op jit(solution)/shard_map/jit(cholesky)/cholesky | solution.py:53
  318.6 10.0 %custom-call.44 = f32[1,128,128]{1,2,0:T(8,128)S(1)} custom-call(f32[1,128,128]{2,1,0:T(8,128)S(1)} %get-tuple-element.11), custom_call_target="InvertDiagBlocksLowerTriangular" | custom-call | tf_op jit(solution)/shard_map/jit(cholesky)/cholesky | solution.py:53
  331.0 11.7 %cholesky.352 = f32[128,128]{1,0:T(8,128)S(1)} custom-call(f32[128,128]{1,0:T(8,128)S(1)} %cholesky.430), custom_call_target="Cholesky" | custom-call | tf_op jit(solution)/shard_map/jit(cholesky)/cholesky | solution.py:53
  342.9 9.8 %custom-call.45 = f32[1,128,128]{1,2,0:T(8,128)S(1)} custom-call(f32[1,128,128]{2,1,0:T(8,128)S(1)} %get-tuple-element.9), custom_call_target="InvertDiagBlocksLowerTriangular" | custom-call | tf_op jit(solution)/shard_map/jit(cholesky)/cholesky | solution.py:53
  355.2 11.9 %cholesky.371 = f32[128,128]{1,0:T(8,128)S(1)} custom-call(f32[128,128]{1,0:T(8,128)S(1)} %cholesky.435), custom_call_target="Cholesky" | custom-call | tf_op jit(solution)/shard_map/jit(cholesky)/cholesky | solution.py:53
  367.2 9.8 %custom-call.46 = f32[1,128,128]{1,2,0:T(8,128)S(1)} custom-call(f32[1,128,128]{2,1,0:T(8,128)S(1)} %get-tuple-element.7), custom_call_target="InvertDiagBlocksLowerTriangular" | custom-call | tf_op jit(solution)/shard_map/jit(cholesky)/cholesky | solution.py:53
  379.3 11.7 %cholesky.390 = f32[128,128]{1,0:T(8,128)S(1)} custom-call(f32[128,128]{1,0:T(8,128)S(1)} %cholesky.440), custom_call_target="Cholesky" | custom-call | tf_op jit(solution)/shard_map/jit(cholesky)/cholesky | solution.py:53
  391.2 9.8 %custom-call.47 = f32[1,128,128]{1,2,0:T(8,128)S(1)} custom-call(f32[1,128,128]{2,1,0:T(8,128)S(1)} %get-tuple-element.5), custom_call_target="InvertDiagBlocksLowerTriangular" | custom-call | tf_op jit(solution)/shard_map/jit(cholesky)/cholesky | solution.py:53
  403.1 11.7 %cholesky.408 = f32[128,128]{1,0:T(8,128)S(1)} custom-call(f32[128,128]{1,0:T(8,128)S(1)} %convolution_subtract_fusion.4), custom_call_target="Cholesky" | custom-call | tf_op jit(solution)/shard_map/jit(cholesky)/cholesky | solution.py:53
  422.9 2.1 convolution_bitcast_fusion
  (63 shorter events, 23.3 us)
Async XLA Ops:
  7.2 415.7 %copy-start = (bf16[1,768,256]{2,1,0:T(8,128)(2,1)S(1)}, bf16[1,768,256]{2,1,0:T(8,128)(2,1)}, u32[]{:S(2)}) copy-start(bf16[1,768,256]{2,1,0:T(8,128)(2,1)} %param.9) | copy-start | bytes 1179652
  7.2 65.8 %all-gather.7.cloned.1.call-start = ((), (), s32[]{:S(2)}) async-start(), calls=%async_computation.3 | async-start | bytes 3538944 | tf_op jit(solution)/shard_map/all_gather | solution.py:47
  7.9 5.0 %copy-start.3 = (s32[8,1]{0,1:T(1,128)S(1)}, s32[8,1]{0,1:T(1,128)}, u32[]{:S(2)}) copy-start(s32[8,1]{0,1:T(1,128)} %param.6) | copy-start | bytes 100
  20.3 99.5 %all-to-all-start = ((bf16[4,1,4,128,2048]{4,3,2,1,0:T(8,128)(2,1)}), bf16[4,1,4,128,2048]{4,3,2,1,0:T(8,128)(2,1)}, u32[]{:S(2)}, u32[]{:S(2)}) async-start(bf16[4,1,4,128,2048]{4,3,2,1,0:T(8,128)(2,1)} %bitcast.58), calls=%async_computation | async-start | bytes 16777216 | tf_op jit(solution)/shard_map/all_to_all | solution.py:36
  25.9 107.9 %all-gather.5.cloned.1.call-start = ((), (), s32[]{:S(2)}) async-start(), calls=%async_computation.2 | async-start | bytes 3538944 | tf_op jit(solution)/shard_map/all_gather | solution.py:42
  26.7 245.3 %all-reduce.4.cloned.1.call-start = ((), (), s32[]{:S(2)}) async-start(), calls=%async_computation.1 | async-start | bytes 4718592 | tf_op jit(solution)/shard_map/psum | solution.py:52
  133.8 10.3 %copy-start.4 = (f32[2048,768]{1,0:T(8,128)S(1)}, f32[2048,768]{1,0:T(8,128)}, u32[]{:S(2)}) copy-start(f32[2048,768]{1,0:T(8,128)} %fusion.7) | copy-start | bytes 18874372
  275.2 3.2 copy-start.1
  280.4 1.4 copy-start.2
Sparse Core Ops, SparseCore 0:
  10.2 62.7 all-gather.6
  75.1 58.6 all-gather.4
  164.4 107.5 all-reduce.3
where the time goes:
time: 438 us; the launch traced here: 433 us
  waiting for transfers between devices  204 us (47%)
  other arithmetic  130 us (30%)
  matrix products  56.5 us (13%)
  between operations  18.3 us (4%)
  local copies, waits for them, and re-layouts  18.2 us (4%)
  starting transfers between devices  5.77 us (1%)
    another operation x23, other arithmetic, on_device(): upper = jnp.linalg.cholesky(total).T  124 us
    psum x1, waiting for transfers between devices, on_device(): total = lax.psum(gram, 'dp') + damping * eye  108 us
    all_to_all x1, waiting for transfers between devices, on_device(): lax.all_to_all(outgoing, 'expert', split_axis=0, concat_axis=0, tiled=True)  46.9 us
    all_gather x1, waiting for transfers between devices, on_device(): lax.all_gather(up_weight[0], 'dp', axis=0, tiled=True)  46.2 us
    dot_general x1, matrix products, on_device(): jnp.dot(hidden.T, hidden, precision=lax.Precision.HIGHEST) / float(rows_avg)  20.1 us
    another operation x10, matrix products, on_device(): upper = jnp.linalg.cholesky(total).T  12.3 us
    dot_general x1, matrix products, on_device(): jnp.dot(rows, lax.all_gather(up_weight[0], 'dp', axis=0, tiled=True), pre...  11.7 us
    dot_general x1, matrix products, on_device(): jnp.dot(rows, lax.all_gather(gate_weight[0], 'dp', axis=0, tiled=True), p...  10.3 us
  transfers between devices with their start and end apart: 4, of which 4 were waited for; matrix products, arithmetic and copies ran while one was open for 6% of the time, Pallas kernels for 0%

commit v1 on v0

--- a/solution.py
+++ b/solution.py
@@ -1,12 +1,143 @@
+import functools
 import jax
 import jax.numpy as jnp
 from jax import lax
+from jax.experimental import pallas as pl
+from jax.experimental.pallas import tpu as pltpu
 from jax.sharding import PartitionSpec as P
 
 BROWS = 128
+NB = 128
+PIVOTS = 8
+HIGHEST = lax.Precision.HIGHEST
 
 
 damping = 0.05
+
+
+def factor_block(rows):
+    q = PIVOTS
+    groups = NB // 8
+    left = list(rows)
+    lane = lax.broadcasted_iota(jnp.int32, (8, NB), 1)
+    sub = lax.broadcasted_iota(jnp.int32, (8, NB), 0)
+    right = [jnp.where(lane == sub + 8 * g, 1.0, 0.0).astype(jnp.float32) for g in range(groups)]
+
+    def spread(x):
+        return jnp.broadcast_to(x, (8, NB))
+
+    for t in range(NB // q):
+        j0 = t * q
+        g, s0 = j0 // 8, j0 % 8
+        p1, p2 = left[g], right[g]
+        a = {}
+        for i in range(q):
+            for k in range(i, q):
+                a[i, k] = spread(p1[s0 + i : s0 + i + 1, j0 + k : j0 + k + 1])
+        r1 = [spread(p1[s0 + i : s0 + i + 1, :]) for i in range(q)]
+        r2 = [spread(p2[s0 + i : s0 + i + 1, :]) for i in range(q)]
+        inv, rs = [], []
+        for c in range(q):
+            root = lax.rsqrt(a[c, c])
+            rs.append(root)
+            inv.append(root * root)
+            for i in range(c + 1, q):
+                m = a[c, i] * inv[c]
+                for k in range(i, q):
+                    a[i, k] = a[i, k] - m * a[c, k]
+                r1[i] = r1[i] - m * r1[c]
+                r2[i] = r2[i] - m * r2[c]
+        for below in range(g, groups):
+            if below == g and s0 + q == 8:
+                continue
+            x1, x2 = left[below], right[below]
+            cols = [spread(x1[:, j0 + c : j0 + c + 1]) for c in range(q)]
+            for c in range(q):
+                tc = cols[c] * inv[c]
+                for k in range(c + 1, q):
+                    cols[k] = cols[k] - tc * a[c, k]
+                if below == g:
+                    tc = jnp.where(sub >= s0 + q, tc, 0.0)
+                x1 = x1 - tc * r1[c]
+                x2 = x2 - tc * r2[c]
+            left[below], right[below] = x1, x2
+        x1, x2 = left[g], right[g]
+        for c in range(q):
+            x1 = jnp.where(sub == s0 + c, r1[c] * rs[c], x1)
+            x2 = jnp.where(sub == s0 + c, r2[c] * rs[c], x2)
+        left[g], right[g] = x1, x2
+    return left, right
+
+
+def split3(x):
+    first = x.astype(jnp.bfloat16)
+    rest = x - first.astype(jnp.float32)
+    second = rest.astype(jnp.bfloat16)
+    third = (rest - second.astype(jnp.float32)).astype(jnp.bfloat16)
+    return first, second, third
+
+
+def factor_kernel(place_ref, gram_ref, down_ref, mine_ref, product_ref, work, inverse):
+    width = gram_ref.shape[0]
+    my_rows = mine_ref.shape[0]
+    count = width // NB
+    work[...] = gram_ref[...]
+    sub = lax.broadcasted_iota(jnp.int32, (8, NB), 0)
+    lane = lax.broadcasted_iota(jnp.int32, (8, NB), 1)
+
+    def step(kb, carry):
+        off = pl.multiple_of(kb * NB, NB)
+        rows = [work[pl.ds(off + 8 * i, 8), pl.ds(off, NB)] for i in range(NB // 8)]
+        upper, low_inv = factor_block(rows)
+        for i in range(NB // 8):
+            work[pl.ds(off + 8 * i, 8), pl.ds(off, NB)] = jnp.where(lane >= sub + 8 * i, upper[i], 0.0)
+            inverse[8 * i : 8 * i + 8, :] = low_inv[i]
+        for k in range(count):
+            @pl.when(kb == k)
+            def _():
+                at, lo = k * NB, (k + 1) * NB
+                if k < count - 1:
+                    panel = jnp.dot(
+                        inverse[...], work[at:lo, lo:], precision=HIGHEST, preferred_element_type=jnp.float32
+                    )
+                    work[at:lo, lo:] = panel
+                    work[lo:, at:lo] = jnp.zeros((width - lo, NB), jnp.float32)
+                    for i in range(k + 1, count):
+                        a = i * NB
+                        work[a : a + NB, a:] -= lax.dot_general(
+                            panel[:, a - lo : a - lo + NB],
+                            panel[:, a - lo :],
+                            (((0,), (0,)), ((), ())),
+                            precision=HIGHEST,
+                            preferred_element_type=jnp.float32,
+                        )
+                down = down_ref[at:, :]
+                parts = [
+                    jnp.dot(piece, down, preferred_element_type=jnp.float32)
+                    for piece in split3(work[at:lo, at:])
+                ]
+                product_ref[at:lo, :] = parts[0] + (parts[1] + parts[2])
+        return carry
+
+    lax.fori_loop(0, count, step, 0)
+    start = pl.multiple_of(place_ref[0] * my_rows, 8)
+    mine_ref[...] = work[pl.ds(start, my_rows), :]
+
+
+def factor_and_product(gram, down, place, my_rows):
+    width = gram.shape[0]
+    vmem = pl.BlockSpec(memory_space=pltpu.VMEM)
+    return pl.pallas_call(
+        factor_kernel,
+        out_shape=(
+            jax.ShapeDtypeStruct((my_rows, width), jnp.float32),
+            jax.ShapeDtypeStruct((width, down.shape[1]), jnp.float32),
+        ),
+        in_specs=[pl.BlockSpec(memory_space=pltpu.SMEM), vmem, vmem],
+        out_specs=(vmem, vmem),
+        scratch_shapes=[pltpu.VMEM((width, width), jnp.float32), pltpu.VMEM((NB, NB), jnp.float32)],
+        name="factor",
+    )(place, gram, down)
 
 
 def on_device(tokens, block_expert, gate_weight, up_weight, down_weight):
@@ -50,10 +181,9 @@
     hidden = jax.nn.silu(gate) * lifted
     gram = jnp.dot(hidden.T, hidden, precision=lax.Precision.HIGHEST) / float(rows_avg)
     total = lax.psum(gram, "dp") + damping * eye
-    upper = jnp.linalg.cholesky(total).T
-    factors = [lax.dynamic_slice_in_dim(upper, lax.axis_index("dp") * my_rows, my_rows, 0)]
-    products = [jnp.dot(upper, down_weight[0].astype(jnp.float32), precision=lax.Precision.HIGHEST)]
-    return (jnp.stack(factors), jnp.stack(products))
+    place = jnp.reshape(lax.axis_index("dp"), (1,)).astype(jnp.int32)
+    mine, product = factor_and_product(total, down_weight[0], place, my_rows)
+    return (mine[None], product[None])
 
 
 def solution(mesh):

time: 438 us -> 314 us (0.72); the launches traced: 433 us -> 314 us
  other arithmetic: 130 us -> 3.52 us
  Pallas kernels: 0 us -> 33.5 us
  matrix products: 56.5 us -> 41.2 us
  local copies, waits for them, and re-layouts: 18.2 us -> 12.1 us
  between operations: 18.3 us -> 13.8 us
    another operation x23 -> x0, other arithmetic: 124 us -> none  [on_device(): upper = jnp.linalg.cholesky(total).T]
    pallas_call x0 -> x1, Pallas kernels: none -> 33.5 us  [factor_and_product(): pl.pallas_call(factor_kernel, out_shape=(jax.ShapeDtypeStruct((my_rows, w...]
    another operation x10 -> x0, matrix products: 12.3 us -> none  [on_device(): upper = jnp.linalg.cholesky(total).T]
  transfers between devices with their start and end apart: 4 -> 4, of which waited for: 4 -> 4; matrix products, arithmetic and copies ran while one was open for 6% -> 8% of each run, Pallas kernels for 0% -> 0%
where the time goes in v1:
time: 314 us
  waiting for transfers between devices  204 us (65%)
  matrix products  41.2 us (13%)
  Pallas kernels  33.5 us (11%)
  between operations  13.8 us (4%)
  local copies, waits for them, and re-layouts  12.1 us (4%)
  starting transfers between devices  5.75 us (2%)
  other arithmetic  3.52 us (1%)
    psum x1, waiting for transfers between devices, on_device(): total = lax.psum(gram, 'dp') + damping * eye  108 us
    all_to_all x1, waiting for transfers between devices, on_device(): lax.all_to_all(outgoing, 'expert', split_axis=0, concat_axis=0, tiled=True)  46.8 us
    all_gather x1, waiting for transfers between devices, on_device(): lax.all_gather(up_weight[0], 'dp', axis=0, tiled=True)  46.2 us
    pallas_call x1, Pallas kernels, factor_and_product(): pl.pallas_call(factor_kernel, out_shape=(jax.ShapeDtypeStruct((my_rows, w...  33.5 us
    dot_general x1, matrix products, on_device(): jnp.dot(hidden.T, hidden, precision=lax.Precision.HIGHEST) / float(rows_avg)  19.1 us
    dot_general x1, matrix products, on_device(): jnp.dot(rows, lax.all_gather(up_weight[0], 'dp', axis=0, tiled=True), pre...  11.7 us
    dot_general x1, matrix products, on_device(): jnp.dot(rows, lax.all_gather(gate_weight[0], 'dp', axis=0, tiled=True), p...  10.3 us
    gather x1, local copies, waits for them, and re-layouts, on_device(): padded[source].reshape(n_expert, exp_local, capacity, BROWS, model)  7.09 us
  transfers between devices with their start and end apart: 4, of which 4 were waited for; matrix products, arithmetic and copies ran while one was open for 8% of the time, Pallas kernels for 0%

profile of v1, /device:TPU:0, one launch (start us, length us, event | category | flops | bytes accessed | tf_op | source)
XLA Modules:
  0.0 314.1 jit_solution(8656208261072176299)
XLA Ops:
  7.2 0.0 copy-start
  7.2 0.0 all-gather.7.cloned.1.call-start
  7.2 0.7 all-gather.7.cloned.1.call-update
  7.9 5.0 %concatenate.3 = bf16[9,128,2048]{2,1,0:T(8,128)(2,1)} pad(bf16[8,128,2048]{2,1,0:T(8,128)(2,1)} %bitcast.21, bf16[]{:T(256)} %constant.42.clone.1), padding=0_1x0_0x0_0 | pad | bytes 8912898 | tf_op jit(solution)/shard_map/concatenate | solution.py:165
  12.9 0.0 copy-done
  12.9 0.2 convert_reduce_fusion.1
  13.1 0.1 convert_reduce_fusion
  13.2 7.1 %gather_fusion = bf16[16,128,2048]{2,1,0:T(8,128)(2,1)} fusion(bf16[9,128,2048]{2,1,0:T(8,128)(2,1)} %concatenate.3, s32[1024]{0:T(1024)S(1)} %pad_clamp_fusion), kind=kCustom, calls=%fused_computation | custom fusion | bytes 16777280 | tf_op jit(solution)/shard_map/gather | solution.py:166
  20.3 5.6 %all-to-all-start = ((bf16[4,1,4,128,2048]{4,3,2,1,0:T(8,128)(2,1)}), bf16[4,1,4,128,2048]{4,3,2,1,0:T(8,128)(2,1)}, u32[]{:S(2)}, u32[]{:S(2)}) async-start(bf16[4,1,4,128,2048]{4,3,2,1,0:T(8,128)(2,1)} %bitcast.20), calls=%async_computation | async-start | bytes 16777216 | tf_op jit(solution)/shard_map/all_to_all | solution.py:167
  25.9 0.0 all-gather.5.cloned.1.call-start
  25.9 0.7 all-gather.5.cloned.1.call-update
  26.6 0.0 all-reduce.3.cloned.1.call-start
  26.7 46.2 %all-gather.7.cloned.1.call-done = bf16[1,2048,768]{2,1,0:T(8,128)(2,1)} async-done(((bf16[1,256,768]{2,1,0:T(8,128)(2,1)}), bf16[1,2048,768]{2,1,0:T(8,128)(2,1)}) %all-gather.7.cloned.1.call-update) | async-done | bytes 3145744 | tf_op jit(solution)/shard_map/all_gather | solution.py:178
  72.9 46.8 %all-to-all-done = bf16[4,1,4,128,2048]{4,3,2,1,0:T(8,128)(2,1)} async-done(((bf16[4,1,4,128,2048]{4,3,2,1,0:T(8,128)(2,1)}), bf16[4,1,4,128,2048]{4,3,2,1,0:T(8,128)(2,1)}, u32[]{:S(2)}, u32[]{:S(2)}) %all-to-all-start) | async-done | bytes 8388640 | tf_op jit(solution)/shard_map/all_to_all | solution.py:167
  119.7 11.7 %fusion.7 = f32[2048,768]{1,0:T(8,128)} fusion(bf16[2048,2048]{1,0:T(8,128)(2,1)} %bitcast.6, bf16[1,2048,768]{2,1,0:T(8,128)(2,1)} %all-gather.7.cloned.1.call-done), kind=kOutput, calls=%fused_computation.8 | convolution fusion | flops 6442450944 | bytes 17825792 | tf_op jit(solution)/shard_map/dot_general | solution.py:176
  131.5 2.4 all-gather.5.cloned.1.call-done
  133.8 0.0 copy-start.1
  133.8 10.3 %fusion.9 = f32[2048,768]{1,0:T(8,128)S(1)} fusion(bf16[2048,2048]{1,0:T(8,128)(2,1)} %bitcast.6, bf16[1,2048,768]{2,1,0:T(8,128)(2,1)} %all-gather.5.cloned.1.call-done), kind=kOutput, calls=%fused_computation.10 | convolution fusion | flops 6442450944 | bytes 17825792 | tf_op jit(solution)/shard_map/dot_general | solution.py:171
  144.2 0.0 copy-done.1
  144.2 19.1 %fusion.12 = f32[768,768]{1,0:T(8,128)} fusion(f32[2048,768]{1,0:T(8,128)S(1)} %copy-done.1, f32[2048,768]{1,0:T(8,128)S(1)} %fusion.9), kind=kOutput, calls=%fused_computation.15 | convolution fusion | flops 14503968768 | bytes 14942208 | tf_op jit(solution)/shard_map/dot_general | solution.py:182
  163.3 0.0 all-reduce.3.cloned.1.call-update
  163.3 107.6 %all-reduce.3.cloned.1.call-done = f32[768,768]{1,0:T(8,128)} async-done(((f32[768,768]{1,0:T(8,128)}), f32[768,768]{1,0:T(8,128)}) %all-reduce.3.cloned.1.call-update) | async-done | bytes 2359312 | tf_op jit(solution)/shard_map/psum | solution.py:183
  270.9 3.2 %select_add_fusion.gram_ref = f32[768,768]{1,0:T(8,128)} fusion(f32[768,768]{1,0:T(8,128)} %all-reduce.3.cloned.1.call-done), kind=kLoop, calls=%fused_computation.13 | loop fusion | flops 1769472 | bytes 4718592 | tf_op jit(solution)/shard_map/add | solution.py:183
  274.2 33.5 %factor.1 = (f32[96,768]{1,0:T(8,128)}, f32[768,256]{1,0:T(8,128)}) custom-call(s32[1]{0:T(128)} %bitcast.place_ref, f32[768,768]{1,0:T(8,128)} %select_add_fusion.gram_ref, bf16[768,256]{1,0:T(8,128)(2,1)} %bitcast.22), custom_call_target="tpu_custom_call" | custom-call | tf_op jit(solution)/shard_map/factor/pallas_call | solution.py:130
  (3 shorter events, 0.0 us)
Async XLA Ops:
  7.2 5.7 %copy-start = (s32[8,1]{0,1:T(1,128)S(1)}, s32[8,1]{0,1:T(1,128)}, u32[]{:S(2)}) copy-start(s32[8,1]{0,1:T(1,128)} %param.6) | copy-start | bytes 100
  7.2 65.8 %all-gather.7.cloned.1.call-start = ((), (), s32[]{:S(2)}) async-start(), calls=%async_computation.3 | async-start | bytes 3538944 | tf_op jit(solution)/shard_map/all_gather | solution.py:178
  20.3 99.5 %all-to-all-start = ((bf16[4,1,4,128,2048]{4,3,2,1,0:T(8,128)(2,1)}), bf16[4,1,4,128,2048]{4,3,2,1,0:T(8,128)(2,1)}, u32[]{:S(2)}, u32[]{:S(2)}) async-start(bf16[4,1,4,128,2048]{4,3,2,1,0:T(8,128)(2,1)} %bitcast.20), calls=%async_computation | async-start | bytes 16777216 | tf_op jit(solution)/shard_map/all_to_all | solution.py:167
  25.9 107.9 %all-gather.5.cloned.1.call-start = ((), (), s32[]{:S(2)}) async-start(), calls=%async_computation.2 | async-start | bytes 3538944 | tf_op jit(solution)/shard_map/all_gather | solution.py:173
  26.6 244.3 %all-reduce.3.cloned.1.call-start = ((), (), s32[]{:S(2)}) async-start(), calls=%async_computation.1 | async-start | bytes 4718592 | tf_op jit(solution)/shard_map/psum | solution.py:183
  133.8 10.3 %copy-start.1 = (f32[2048,768]{1,0:T(8,128)S(1)}, f32[2048,768]{1,0:T(8,128)}, u32[]{:S(2)}) copy-start(f32[2048,768]{1,0:T(8,128)} %fusion.7) | copy-start | bytes 18874372
Sparse Core Ops, SparseCore 0:
  10.2 62.7 all-gather.6
  75.1 58.6 all-gather.4
  163.4 107.4 all-reduce.2
